TPU v7x, 512 devices: a whole 4x8x8 slice. The times are simulated.
512 devices in a mesh: row: 16 (over x, y_lo), blk: 32 (over y_hi, z, core).
Axes of the slice: x: 4, y: 8 (y_hi: 2, y_lo: 4; y = y_hi * 4 + y_lo), z: 8, core: 2. Of those that a mesh axis runs over, the one named last changes fastest.
Arguments:
- cells: bfloat16 [131072, 768], P(('row', 'blk')), may hold values from -12 to 12
- tile_rows: int32 [6144], P(('row', 'blk')), may hold values from 0 to 1, as said below
- tile_cols: int32 [6144], P(('row', 'blk')), may hold values from 0 to 5, as said below
- tile_count: int32 [512], P(('row', 'blk')), may hold values from 6 to 12, as said below
- halo_blocks: int32 [512], P(('row', 'blk')), may hold values from 0 to 1, as said below
- tile_vals: bfloat16 [6144, 128, 128], P(('row', 'blk')), may hold values from -0.375 to 0.375
- pool_ids: int32 [131072], P(('row', 'blk')), may hold values from 0 to 15, as said below
- w_msg: bfloat16 [768, 768], replicated, may hold values from -0.21875 to 0.21875
- w_query: bfloat16 [768, 768], replicated, may hold values from -1 to 2
- cotangent: bfloat16 [131072, 768], P(('row', 'blk')), may hold values from -6 to 6
Outputs:
- passed: bfloat16 [131072, 768], P(('row', 'blk'))
- attended: bfloat16 [131072, 768], P(('row', 'blk'))
- grad_cells: bfloat16 [131072, 768], P(('row', 'blk'))
Inputs may be any that keep to these rules, and one draw needn't show every extreme that they name: `tile_rows`: slot i of a partition's 12 slots, for i < 2, has row i. `tile_cols`: slot i of a partition, for i < 6, has column i; later slots have columns below 2. `tile_count`: slots of a partition at or beyond its count are unused. `halo_blocks`: distinct within one partition. `pool_ids`: every supernode of a partition has at least one of its cells; the first two cells of a partition lie in supernodes 0 and 1.
All inputs are finite; a program needn't handle non-finite values.
Results may differ from a plain program's by a relative error of at most 0.04.
The roundings to bfloat16 on the way count: a program that leaves them out, or rounds other values in their place, can miss the bound.
Values may be sent and summed in bfloat16 or wider, within the bound.
No kernel may reach another device: no remote copies, remote signals or barrier semaphores. Data moves between devices by JAX's collectives and lax.ppermute only.
A program may use at most 64 MiB of HBM per device.

v0:
```python
import jax
import jax.numpy as jnp
from jax import lax
from jax.sharding import PartitionSpec as P

D = 768
HEADS = 12
HEAD = 64
BLOCK = 128
NB = 2
HB = 1
SN_DEV = 16
EXT = 6
CELL_DEV = 256


def padded(value, sides, width):
    for axis, dim in sides:
        count, length = (lax.axis_size(axis), value.shape[dim])
        up = [(i, (i + 1) % count) for i in range(count - 1)]
        down = [(j, i) for i, j in up]
        last = lax.slice_in_dim(value, length - width, length, axis=dim)
        leading = lax.slice_in_dim(value, 0, width, axis=dim)
        before = lax.ppermute(last, axis, up)
        after = lax.ppermute(leading, axis, down)
        value = jnp.concatenate([before, value, after], axis=dim)
    return value


def passed_along(value, axis, steps):
    count = lax.axis_size(axis)
    leading, last = (max(0, -steps), min(count, count - steps))
    return lax.ppermute(value, axis, [(source, source + steps) for source in range(leading, last)])


def silu_slope(values):
    sigma = jax.nn.sigmoid(values)
    return sigma * (1.0 + values * (1.0 - sigma))


def body(
    cells,
    tile_rows,
    tile_cols,
    tile_count,
    halo_blocks,
    tile_vals,
    pool_ids,
    w_msg,
    w_query,
    cotangent,
):
    blocks = cells.reshape(NB, BLOCK, D)
    boundary = blocks[halo_blocks]
    beside_all = padded(boundary[None, None], (("row", 0), ("blk", 1)), 1)
    extended = jnp.concatenate(
        [blocks, beside_all[0, 1], beside_all[2, 1], beside_all[1, 0], beside_all[1, 2]], axis=0
    )
    live_count = tile_count[0]

    def add_tile(number, totals):
        picked = lax.dynamic_index_in_dim(extended, tile_cols[number], 0, keepdims=False)
        product = jnp.dot(tile_vals[number], picked, preferred_element_type=jnp.float32)
        return totals.at[tile_rows[number]].add(product)

    msg_sums = lax.fori_loop(0, live_count, add_tile, jnp.zeros((NB, BLOCK, D), jnp.float32))
    message = msg_sums.astype(jnp.bfloat16).reshape(CELL_DEV, D)
    hidden = jnp.dot(message, w_msg, preferred_element_type=jnp.float32)
    passed = (cells.astype(jnp.float32) + jax.nn.silu(hidden)).astype(jnp.bfloat16)
    member = pool_ids[None, :] == jnp.arange(SN_DEV, dtype=jnp.int32)[:, None]
    member_bf = member.astype(jnp.bfloat16)
    counts = jnp.sum(member.astype(jnp.float32), axis=1)
    root_count = jnp.sqrt(counts)[:, None]
    pooled = jnp.dot(member_bf, passed, preferred_element_type=jnp.float32)
    supern = (pooled / root_count).astype(jnp.bfloat16)
    query_proj = jnp.dot(passed, w_query, preferred_element_type=jnp.float32).astype(jnp.bfloat16)
    key_table = lax.all_gather(supern, "blk", axis=0, tiled=True)
    score_scale = HEAD ** (-0.5)
    queries = query_proj.reshape(CELL_DEV, HEADS, HEAD)
    key_rows = key_table.reshape(-1, HEADS, HEAD)
    grads = cotangent.reshape(CELL_DEV, HEADS, HEAD)
    scores = (
        jnp.einsum("qhe,khe->hqk", queries, key_rows, preferred_element_type=jnp.float32)
        * score_scale
    )
    weights = jnp.exp(scores - jnp.max(scores, axis=2, keepdims=True))
    weights = weights / jnp.sum(weights, axis=2, keepdims=True)
    rounded = weights.astype(jnp.bfloat16)
    values_sum = jnp.einsum("hqk,khe->qhe", rounded, key_rows, preferred_element_type=jnp.float32)
    centre = jnp.sum(grads.astype(jnp.float32) * values_sum, axis=2)
    slope = jnp.einsum("qhe,khe->hqk", grads, key_rows, preferred_element_type=jnp.float32)
    dscore = (weights * (slope - centre.T[:, :, None]) * score_scale).astype(jnp.bfloat16)
    dquery = (
        jnp.einsum("hqk,khe->qhe", dscore, key_rows, preferred_element_type=jnp.float32)
        .astype(jnp.bfloat16)
        .reshape(CELL_DEV, D)
    )
    from_scores = jnp.einsum("hqk,qhe->khe", dscore, queries, preferred_element_type=jnp.float32)
    from_values = jnp.einsum("hqk,qhe->khe", rounded, grads, preferred_element_type=jnp.float32)
    key_grad = lax.psum_scatter(
        (from_scores + from_values).reshape(lax.axis_size("blk") * SN_DEV, D),
        "blk",
        scatter_dimension=0,
        tiled=True,
    )
    pool_grad = (key_grad / root_count).astype(jnp.bfloat16)
    spread = jnp.einsum("sc,sf->cf", member_bf, pool_grad, preferred_element_type=jnp.float32)
    back_query = lax.dot_general(
        dquery, w_query, (((1,), (1,)), ((), ())), preferred_element_type=jnp.float32
    )
    through = (cotangent.astype(jnp.float32) + back_query + spread).astype(jnp.bfloat16)
    dhidden = (through.astype(jnp.float32) * silu_slope(hidden)).astype(jnp.bfloat16)
    dmessage = (
        lax.dot_general(
            dhidden, w_msg, (((1,), (1,)), ((), ())), preferred_element_type=jnp.float32
        )
        .astype(jnp.bfloat16)
        .reshape(NB, BLOCK, D)
    )

    def back_tile(number, totals):
        picked = lax.dynamic_index_in_dim(dmessage, tile_rows[number], 0, keepdims=False)
        product = lax.dot_general(
            tile_vals[number], picked, (((0,), (0,)), ((), ())), preferred_element_type=jnp.float32
        )
        return totals.at[tile_cols[number]].add(product)

    ext_grad = lax.fori_loop(0, live_count, back_tile, jnp.zeros((EXT, BLOCK, D), jnp.float32))
    returned = jnp.zeros((HB, BLOCK, D), jnp.float32)
    for offset, first_slot in ((1, NB + HB), (-1, NB)):
        returned = returned + passed_along(ext_grad[first_slot : first_slot + HB], "row", offset)
    for offset, first_slot in ((1, NB + 3 * HB), (-1, NB + 2 * HB)):
        returned = returned + passed_along(ext_grad[first_slot : first_slot + HB], "blk", offset)
    summed = through.astype(jnp.float32).reshape(NB, BLOCK, D) + ext_grad[:NB]
    summed = summed.at[halo_blocks].add(returned)
    attended = values_sum.astype(jnp.bfloat16).reshape(CELL_DEV, D)
    return (passed, attended, summed.astype(jnp.bfloat16).reshape(CELL_DEV, D))


def solution(mesh):
    return jax.shard_map(
        body,
        mesh=mesh,
        in_specs=(
            P(("row", "blk"), None),
            P(("row", "blk")),
            P(("row", "blk")),
            P(("row", "blk")),
            P(("row", "blk")),
            P(("row", "blk"), None, None),
            P(("row", "blk")),
            P(),
            P(),
            P(("row", "blk"), None),
        ),
        out_specs=(P(("row", "blk"), None), P(("row", "blk"), None), P(("row", "blk"), None)),
        check_vma=False,
    )
```

profile of v0, /device:TPU:1, one launch (start us, length us, event | category | flops | bytes accessed | tf_op | source)
XLA Modules:
  0.0 499.1 jit_solution(8271028985176664791)
XLA Ops:
  9.0 4.0 collective-permute-start
  16.5 8.1 %collective-permute-done.1 = bf16[1,1,1,128,768]{4,3,2,1,0:T(8,128)(2,1)S(1)} collective-permute-done((bf16[1,1,1,128,768]{4,3,2,1,0:T(8,128)(2,1)S(1)}, bf16[1,1,1,128,768]{4,3,2,1,0:T(8,128)(2,1)S(1)}, u32[]{:S(2)}, u32[]{:S(2)}) %collective-permute-start.1) | collective-permute-done | bytes 196640 | tf_op jit(solution)/shard_map/ppermute | solution.py:25
  24.6 5.3 %collective-permute-start.2 = (bf16[3,1,1,128,768]{4,3,2,1,0:T(8,128)(2,1)S(1)}, bf16[3,1,1,128,768]{4,3,2,1,0:T(8,128)(2,1)S(1)}, u32[]{:S(2)}, u32[]{:S(2)}) collective-permute-start(bf16[3,1,1,128,768]{4,3,2,1,0:T(8,128)(2,1)S(1)} %pad_maximum_fusion), channel_id=1, source_target_pairs={{0,1},{1,2},{2,3},{3,4},{4,5},{5,6},{6,7},{7,8},{8,9},{9,10},{10,1... | collective-permute-start | bytes 1769480 | tf_op jit(solution)/shard_map/ppermute | solution.py:24
  29.9 1.9 collective-permute-start.3
  31.9 4.8 collective-permute-done.2
  36.7 4.4 collective-permute-done.3
  41.2 48.9 %while.24 = (s32[]{:T(128)}, f32[2,128,768]{2,1,0:T(8,128)S(1)}, s32[]{:T(128)}, s32[12]{0:T(128)S(1)}, bf16[12,128,128]{2,1,0:T(8,128)(2,1)}, /*index=5*/s32[12...) while((s32[]{:T(128)}, f32[2,128,768]{2,1,0:T(8,128)S(1)}, ...), condition=%wide.region_2.3_spmd, body=%wide.region_0.2_spmd.sunk | while | flops 25362460 | bytes 1017128 | solution.py:66
  90.3 2.4 add_convert_fusion
  93.4 105.0 %all_gather.3 = bf16[512,768]{1,0:T(8,128)(2,1)} all-gather(bf16[16,768]{1,0:T(8,128)(2,1)S(1)} %fusion.26), channel_id=1, replica_groups=mesh['row'=16,'blk'=32] {'blk'}, dimensions={0}, use_global_device_ids=true | all-gather | bytes 811008 | tf_op jit(solution)/shard_map/all_gather | solution.py:77
  199.8 2.2 convolution_convert_fusion.2
  203.2 4.6 fusion.39
  207.9 3.3 fusion.23
  218.7 3.1 convolution_convert_fusion.1
  223.2 123.1 %reduce-scatter.2.cloned.1.call-done = f32[16,768]{1,0:T(8,128)} async-done(((f32[512,768]{1,0:T(8,128)}), f32[16,768]{1,0:T(8,128)}) %reduce-scatter.2.cloned.1.call-update) | async-done | bytes 49168 | tf_op jit(solution)/shard_map/reduce_scatter | solution.py:100
  347.9 2.8 convolution_convert_fusion
  351.4 53.5 %while.25 = (s32[]{:T(128)}, f32[6,128,768]{2,1,0:T(8,128)S(1)}, s32[]{:T(128)}, s32[12]{0:T(128)S(1)}, bf16[12,128,128]{2,1,0:T(8,128)(2,1)}, /*index=5*/s32[12...) while((s32[]{:T(128)}, f32[6,128,768]{2,1,0:T(8,128)S(1)}, ...), condition=%wide.region_10.11_spmd, body=%wide.region_8.10_spmd.sunk | while | flops 25362460 | bytes 1017128 | solution.py:128
  367.1 1.9 fusion.74
  406.0 60.6 %collective-permute-start.7 = (f32[1,128,768]{2,1,0:T(8,128)}, f32[1,128,768]{2,1,0:T(8,128)}, u32[]{:S(2)}, u32[]{:S(2)}) collective-permute-start(f32[1,128,768]{2,1,0:T(8,128)} %get-tuple-element.166), channel_id=1, source_target_pairs={{1,0},{2,1},{3,2},{4,3},{5,4},{6,5},{7,6},{8,7},{9,8},{10,9},{11,1... | collective-permute-start | bytes 1179656 | tf_op jit(solution)/shard_map/ppermute | solution.py:33
  466.6 1.9 collective-permute-start.6
  468.5 3.6 collective-permute-start.4
  474.2 1.9 copy.34
  477.3 3.2 collective-permute-done.4
  480.5 8.7 %collective-permute-done.5 = f32[1,128,768]{2,1,0:T(8,128)} collective-permute-done((f32[1,128,768]{2,1,0:T(8,128)}, f32[1,128,768]{2,1,0:T(8,128)}, u32[]{:S(2)}, u32[]{:S(2)}) %collective-permute-start.5) | collective-permute-done | bytes 393248 | tf_op jit(solution)/shard_map/ppermute | solution.py:33
  489.3 2.2 fusion.29
  (115 shorter events, 67.6 us)
Async XLA Ops:
  7.2 83.1 %copy-start = (bf16[768,768]{1,0:T(8,128)(2,1)S(1)}, bf16[768,768]{1,0:T(8,128)(2,1)}, u32[]{:S(2)}) copy-start(bf16[768,768]{1,0:T(8,128)(2,1)} %param.27) | copy-start | bytes 3538948
  7.2 22.7 %copy-start.10 = (bf16[256,768]{1,0:T(8,128)(2,1)S(1)}, bf16[256,768]{1,0:T(8,128)(2,1)}, u32[]{:S(2)}) copy-start(bf16[256,768]{1,0:T(8,128)(2,1)} %param.20) | copy-start | bytes 1179652
  7.2 339.2 %reduce-scatter.2.cloned.1.call-start = ((), (), s32[]{:S(2)}) async-start(), calls=%async_computation.1 | async-start | bytes 1622016 | tf_op jit(solution)/shard_map/reduce_scatter | solution.py:100
  9.0 7.5 %collective-permute-start = (bf16[1,1,1,128,768]{4,3,2,1,0:T(8,128)(2,1)S(1)}, bf16[1,1,1,128,768]{4,3,2,1,0:T(8,128)(2,1)S(1)}, u32[]{:S(2)}, u32[]{:S(2)}) collective-permute-start(bf16[1,1,1,128,768]{4,3,2,1,0:T(8,128)(2,1)S(1)} %dynamic-slice_bitcast_fusion), channel_id=1, source_target_pairs={{0,32},{32,64},{64,96},{96,128},{128,160},{160,192},{192,224},{224... | collective-permute-start | bytes 589832 | tf_op jit(solution)/shard_map/ppermute | solution.py:24
  13.0 11.5 %collective-permute-start.1 = (bf16[1,1,1,128,768]{4,3,2,1,0:T(8,128)(2,1)S(1)}, bf16[1,1,1,128,768]{4,3,2,1,0:T(8,128)(2,1)S(1)}, u32[]{:S(2)}, u32[]{:S(2)}) collective-permute-start(bf16[1,1,1,128,768]{4,3,2,1,0:T(8,128)(2,1)S(1)} %dynamic-slice_bitcast_fusion), channel_id=1, source_target_pairs={{32,0},{64,32},{96,64},{128,96},{160,128},{192,160},{224,192},{256... | collective-permute-start | bytes 589832 | tf_op jit(solution)/shard_map/ppermute | solution.py:25
  15.5 197.6 %copy-start.5 = (bf16[256,768]{0,1:T(8,128)(2,1)}, bf16[256,768]{0,1:T(8,128)(2,1)S(1)}, u32[]{:S(2)}) copy-start(bf16[256,768]{0,1:T(8,128)(2,1)S(1)} %copy.31) | copy-start | bytes 1179652
  15.5 25.7 %copy-start.11 = (s32[3]{0:T(128)S(1)}, s32[3]{0:T(128)}, u32[]{:S(2)}) copy-start(s32[3]{0:T(128)} %constant.110.clone.1) | copy-start | bytes 40
  15.5 25.7 %copy-start.14 = (s32[12]{0:T(128)S(1)}, s32[12]{0:T(128)}, u32[]{:S(2)}) copy-start(s32[12]{0:T(128)} %param.21) | copy-start | bytes 148
  15.5 25.7 %copy-start.15 = (s32[12]{0:T(128)S(1)}, s32[12]{0:T(128)}, u32[]{:S(2)}) copy-start(s32[12]{0:T(128)} %param.22) | copy-start | bytes 148
  24.6 12.1 %collective-permute-start.2 = (bf16[3,1,1,128,768]{4,3,2,1,0:T(8,128)(2,1)S(1)}, bf16[3,1,1,128,768]{4,3,2,1,0:T(8,128)(2,1)S(1)}, u32[]{:S(2)}, u32[]{:S(2)}) collective-permute-start(bf16[3,1,1,128,768]{4,3,2,1,0:T(8,128)(2,1)S(1)} %pad_maximum_fusion), channel_id=1, source_target_pairs={{0,1},{1,2},{2,3},{3,4},{4,5},{5,6},{6,7},{7,8},{8,9},{9,10},{10,1... | collective-permute-start | bytes 1769480 | tf_op jit(solution)/shard_map/ppermute | solution.py:24
  29.9 11.2 %collective-permute-start.3 = (bf16[3,1,1,128,768]{4,3,2,1,0:T(8,128)(2,1)S(1)}, bf16[3,1,1,128,768]{4,3,2,1,0:T(8,128)(2,1)S(1)}, u32[]{:S(2)}, u32[]{:S(2)}) collective-permute-start(bf16[3,1,1,128,768]{4,3,2,1,0:T(8,128)(2,1)S(1)} %pad_maximum_fusion), channel_id=1, source_target_pairs={{1,0},{2,1},{3,2},{4,3},{5,4},{6,5},{7,6},{8,7},{9,8},{10,9},{11,1... | collective-permute-start | bytes 1769480 | tf_op jit(solution)/shard_map/ppermute | solution.py:25
  90.3 2.4 copy-start.13
  92.7 0.7 copy-start.9
  92.7 107.2 %copy-start.3 = (bf16[768,768]{1,0:T(8,128)(2,1)S(1)}, bf16[768,768]{1,0:T(8,128)(2,1)}, u32[]{:S(2)}) copy-start(bf16[768,768]{1,0:T(8,128)(2,1)} %param.28) | copy-start | bytes 3538948
  207.9 5.2 %copy-start.2 = (f32[12,256,512]{2,1,0:T(8,128)S(1)}, f32[12,256,512]{2,1,0:T(8,128)}, u32[]{:S(2)}) copy-start(f32[12,256,512]{2,1,0:T(8,128)} %get-tuple-element.174) | copy-start | bytes 18874372
  214.7 1.6 copy-start.1
  214.8 1.6 copy-start.6
  218.7 3.1 copy-start.4
  218.7 3.1 copy-start.8
  347.9 2.8 copy-start.7
  406.0 71.3 %collective-permute-start.7 = (f32[1,128,768]{2,1,0:T(8,128)}, f32[1,128,768]{2,1,0:T(8,128)}, u32[]{:S(2)}, u32[]{:S(2)}) collective-permute-start(f32[1,128,768]{2,1,0:T(8,128)} %get-tuple-element.166), channel_id=1, source_target_pairs={{1,0},{2,1},{3,2},{4,3},{5,4},{6,5},{7,6},{8,7},{9,8},{10,9},{11,1... | collective-permute-start | bytes 1179656 | tf_op jit(solution)/shard_map/ppermute | solution.py:33
  466.6 10.7 %collective-permute-start.6 = (f32[1,128,768]{2,1,0:T(8,128)}, f32[1,128,768]{2,1,0:T(8,128)}, u32[]{:S(2)}, u32[]{:S(2)}) collective-permute-start(f32[1,128,768]{2,1,0:T(8,128)} %get-tuple-element.167), channel_id=1, source_target_pairs={{0,1},{1,2},{2,3},{3,4},{4,5},{5,6},{6,7},{7,8},{8,9},{9,10},{10,1... | collective-permute-start | bytes 1179656 | tf_op jit(solution)/shard_map/ppermute | solution.py:33
  468.5 12.0 %collective-permute-start.4 = (f32[1,128,768]{2,1,0:T(8,128)}, f32[1,128,768]{2,1,0:T(8,128)}, u32[]{:S(2)}, u32[]{:S(2)}) collective-permute-start(f32[1,128,768]{2,1,0:T(8,128)} %get-tuple-element.168), channel_id=1, source_target_pairs={{0,32},{32,64},{64,96},{96,128},{128,160},{160,192},{192,224},{224... | collective-permute-start | bytes 1179656 | tf_op jit(solution)/shard_map/ppermute | solution.py:33
  472.1 17.2 %collective-permute-start.5 = (f32[1,128,768]{2,1,0:T(8,128)}, f32[1,128,768]{2,1,0:T(8,128)}, u32[]{:S(2)}, u32[]{:S(2)}) collective-permute-start(f32[1,128,768]{2,1,0:T(8,128)} %get-tuple-element.165), channel_id=1, source_target_pairs={{32,0},{64,32},{96,64},{128,96},{160,128},{192,160},{224,192},{256... | collective-permute-start | bytes 1179656 | tf_op jit(solution)/shard_map/ppermute | solution.py:33
  (2 other events, 1.3 us)
Sparse Core Ops, SparseCore 0:
  218.8 127.5 reduce-scatter.1
where the time goes:
time: 503 us; the launch traced here: 499 us
  waiting for transfers between devices  152 us (30%)
  blocking collectives  105 us (21%)
  starting transfers between devices  79.9 us (16%)
  loops' own time  57.3 us (11%)
  matrix products  43.9 us (9%)
  local copies, waits for them, and re-layouts  27 us (5%)
  other arithmetic  18.4 us (4%)
  between operations  15.2 us (3%)
    reduce_scatter x1, waiting for transfers between devices, body(): lax.psum_scatter((from_scores + from_values).reshape(lax.axis_size('blk')...  123 us
    all_gather x1, blocking collectives, body(): key_table = lax.all_gather(supern, 'blk', axis=0, tiled=True)  105 us
    ppermute x4, starting transfers between devices, passed_along(): lax.ppermute(value, axis, [(source, source + steps) for source in range(l...  67.4 us
    another operation x1, loops' own time, body(): lax.fori_loop(0, live_count, back_tile, jnp.zeros((EXT, BLOCK, D), jnp.fl...  29.5 us
    another operation x1, loops' own time, body(): lax.fori_loop(0, live_count, add_tile, jnp.zeros((NB, BLOCK, D), jnp.floa...  27.8 us
    ppermute x2, waiting for transfers between devices, padded(): after = lax.ppermute(leading, axis, down)  12.5 us
    ppermute x4, waiting for transfers between devices, passed_along(): lax.ppermute(value, axis, [(source, source + steps) for source in range(l...  12 us
    dot_general x6, matrix products, back_tile(): lax.dot_general(tile_vals[number], picked, (((0,), (0,)), ((), ())), pref...  11.3 us
  transfers between devices with their start and end apart: 9, of which 6 were waited for; matrix products, arithmetic and copies ran while one was open for 2% of the time, Pallas kernels for 0%

commit v1 on v0

--- a/solution.py
+++ b/solution.py
@@ -74,7 +74,9 @@
     pooled = jnp.dot(member_bf, passed, preferred_element_type=jnp.float32)
     supern = (pooled / root_count).astype(jnp.bfloat16)
     query_proj = jnp.dot(passed, w_query, preferred_element_type=jnp.float32).astype(jnp.bfloat16)
-    key_table = lax.all_gather(supern, "blk", axis=0, tiled=True)
+    key_table = jnp.concatenate(
+        lax.all_to_all(jnp.stack([supern] * lax.axis_size("blk")), "blk", 0, 0), axis=0
+    )
     score_scale = HEAD ** (-0.5)
     queries = query_proj.reshape(CELL_DEV, HEADS, HEAD)
     key_rows = key_table.reshape(-1, HEADS, HEAD)

time: 503 us -> 473 us (0.940)
  blocking collectives: 105 us -> 0 us
  starting transfers between devices: 79.9 us -> 137 us
  waiting for transfers between devices: 152 us -> 175 us
    all_gather x1 -> x0, blocking collectives: 105 us -> none  [body(): key_table = lax.all_gather(supern, 'blk', axis=0, tiled=True)]
    all_to_all x0 -> x1, starting transfers between devices: none -> 63.2 us  [body(): lax.all_to_all(jnp.stack([supern] * lax.axis_size('blk')), 'blk', 0, 0)]
    all_to_all x0 -> x1, waiting for transfers between devices: none -> 18.8 us  [body(): lax.all_to_all(jnp.stack([supern] * lax.axis_size('blk')), 'blk', 0, 0)]
    another operation x0 -> x3, local copies, waits for them, and re-layouts: none -> 5.93 us  [the longest x2 4.93 us: body(): key_rows = key_table.reshape(-1, HEADS, HEAD)]
    ppermute x4, starting transfers between devices: 67.4 us -> 61.5 us  [passed_along(): lax.ppermute(value, axis, [(source, source + steps) for source in range(l...]
  transfers between devices with their start and end apart: 9 -> 10, of which waited for: 6 -> 8; matrix products, arithmetic and copies ran while one was open for 2% -> 2% of each run, Pallas kernels for 0% -> 0%
where the time goes in v1:
time: 473 us; the launch traced here: 469 us
  waiting for transfers between devices  175 us (37%)
  starting transfers between devices  137 us (29%)
  loops' own time  53.6 us (11%)
  matrix products  40.5 us (9%)
  local copies, waits for them, and re-layouts  30.5 us (6%)
  other arithmetic  17.5 us (4%)
  between operations  15.2 us (3%)
    reduce_scatter x1, waiting for transfers between devices, body(): lax.psum_scatter((from_scores + from_values).reshape(lax.axis_size('blk')...  125 us
    all_to_all x1, starting transfers between devices, body(): lax.all_to_all(jnp.stack([supern] * lax.axis_size('blk')), 'blk', 0, 0)  63.2 us
    ppermute x4, starting transfers between devices, passed_along(): lax.ppermute(value, axis, [(source, source + steps) for source in range(l...  61.5 us
    another operation x1, loops' own time, body(): lax.fori_loop(0, live_count, add_tile, jnp.zeros((NB, BLOCK, D), jnp.floa...  28.1 us
    another operation x1, loops' own time, body(): lax.fori_loop(0, live_count, back_tile, jnp.zeros((EXT, BLOCK, D), jnp.fl...  25.5 us
    all_to_all x1, waiting for transfers between devices, body(): lax.all_to_all(jnp.stack([supern] * lax.axis_size('blk')), 'blk', 0, 0)  18.8 us
    ppermute x2, waiting for transfers between devices, padded(): after = lax.ppermute(leading, axis, down)  14.4 us
    ppermute x4, waiting for transfers between devices, passed_along(): lax.ppermute(value, axis, [(source, source + steps) for source in range(l...  12 us
  transfers between devices with their start and end apart: 10, of which 8 were waited for; matrix products, arithmetic and copies ran while one was open for 2% of the time, Pallas kernels for 0%

profile of v1, /device:TPU:1, one launch (start us, length us, event | category | flops | bytes accessed | tf_op | source)
XLA Modules:
  0.0 469.2 jit_solution(1364602197057019336)
XLA Ops:
  8.9 4.0 collective-permute-start
  15.5 8.9 %collective-permute-done.1 = bf16[1,1,1,128,768]{4,3,2,1,0:T(8,128)(2,1)S(1)} collective-permute-done((bf16[1,1,1,128,768]{4,3,2,1,0:T(8,128)(2,1)S(1)}, bf16[1,1,1,128,768]{4,3,2,1,0:T(8,128)(2,1)S(1)}, u32[]{:S(2)}, u32[]{:S(2)}) %collective-permute-start.1) | collective-permute-done | bytes 196640 | tf_op jit(solution)/shard_map/ppermute | solution.py:25
  24.6 5.3 %collective-permute-start.2 = (bf16[3,1,1,128,768]{4,3,2,1,0:T(8,128)(2,1)S(1)}, bf16[3,1,1,128,768]{4,3,2,1,0:T(8,128)(2,1)S(1)}, u32[]{:S(2)}, u32[]{:S(2)}) collective-permute-start(bf16[3,1,1,128,768]{4,3,2,1,0:T(8,128)(2,1)S(1)} %pad_maximum_fusion), channel_id=1, source_target_pairs={{0,1},{1,2},{2,3},{3,4},{4,5},{5,6},{6,7},{7,8},{8,9},{9,10},{10,1... | collective-permute-start | bytes 1769480 | tf_op jit(solution)/shard_map/ppermute | solution.py:24
  30.9 1.9 collective-permute-start.3
  32.9 3.8 collective-permute-done.2
  36.7 5.4 %collective-permute-done.3 = bf16[3,1,1,128,768]{4,3,2,1,0:T(8,128)(2,1)S(1)} collective-permute-done((bf16[3,1,1,128,768]{4,3,2,1,0:T(8,128)(2,1)S(1)}, bf16[3,1,1,128,768]{4,3,2,1,0:T(8,128)(2,1)S(1)}, u32[]{:S(2)}, u32[]{:S(2)}) %collective-permute-start.3) | collective-permute-done | bytes 589856 | tf_op jit(solution)/shard_map/ppermute | solution.py:25
  42.2 49.0 %while.24 = (s32[]{:T(128)}, f32[2,128,768]{2,1,0:T(8,128)S(1)}, s32[]{:T(128)}, s32[12]{0:T(128)S(1)}, bf16[12,128,128]{2,1,0:T(8,128)(2,1)}, /*index=5*/s32[12...) while((s32[]{:T(128)}, f32[2,128,768]{2,1,0:T(8,128)S(1)}, ...), condition=%wide.region_2.3_spmd, body=%wide.region_0.2_spmd.sunk | while | flops 25362460 | bytes 1017128 | solution.py:66
  93.9 63.2 %all-to-all-start = ((bf16[32,16,768]{2,1,0:T(8,128)(2,1)}), bf16[32,16,768]{2,1,0:T(8,128)(2,1)}, u32[]{:S(2)}, u32[]{:S(2)}) async-start(bf16[32,16,768]{2,1,0:T(8,128)(2,1)} %stack.2), calls=%async_computation | async-start | bytes 1572864 | tf_op jit(solution)/shard_map/all_to_all | solution.py:78
  159.4 18.8 %all-to-all-done = bf16[32,16,768]{2,1,0:T(8,128)(2,1)} async-done(((bf16[32,16,768]{2,1,0:T(8,128)(2,1)}), bf16[32,16,768]{2,1,0:T(8,128)(2,1)}, u32[]{:S(2)}, u32[]{:S(2)}) %all-to-all-start) | async-done | bytes 786464 | tf_op jit(solution)/shard_map/all_to_all | solution.py:78
  178.3 2.7 reshape_reshape.3
  181.0 2.2 copy.31
  183.2 5.9 %fusion.39 = (f32[12,256]{1,0:T(8,128)S(1)}, f32[12,256,512]{2,1,0:T(8,128)}) fusion(bf16[256,12,64]{0,2,1:T(8,128)(2,1)} %bitcast.128, bf16[512,12,64]{0,2,1:T(8,128)(2,1)} %copy.31), kind=kOutput, calls=%fused_computation.69 | convolution fusion | flops 206045696 | bytes 7483392 | tf_op jit(solution)/shard_map/sub | solution.py:88
  189.1 3.3 fusion.23
  199.9 3.1 convolution_convert_fusion.1
  203.5 125.2 %reduce-scatter.2.cloned.1.call-done = f32[16,768]{1,0:T(8,128)} async-done(((f32[512,768]{1,0:T(8,128)}), f32[16,768]{1,0:T(8,128)}) %reduce-scatter.2.cloned.1.call-update) | async-done | bytes 49168 | tf_op jit(solution)/shard_map/reduce_scatter | solution.py:102
  329.9 2.8 convolution_convert_fusion
  333.4 47.5 %while.25 = (s32[]{:T(128)}, f32[6,128,768]{2,1,0:T(8,128)S(1)}, s32[]{:T(128)}, s32[12]{0:T(128)S(1)}, bf16[12,128,128]{2,1,0:T(8,128)(2,1)}, /*index=5*/s32[12...) while((s32[]{:T(128)}, f32[6,128,768]{2,1,0:T(8,128)S(1)}, ...), condition=%wide.region_10.11_spmd, body=%wide.region_8.10_spmd.sunk | while | flops 25362460 | bytes 1017128 | solution.py:130
  382.1 54.7 %collective-permute-start.7 = (f32[1,128,768]{2,1,0:T(8,128)}, f32[1,128,768]{2,1,0:T(8,128)}, u32[]{:S(2)}, u32[]{:S(2)}) collective-permute-start(f32[1,128,768]{2,1,0:T(8,128)} %get-tuple-element.166), channel_id=1, source_target_pairs={{1,0},{2,1},{3,2},{4,3},{5,4},{6,5},{7,6},{8,7},{9,8},{10,9},{11,1... | collective-permute-start | bytes 1179656 | tf_op jit(solution)/shard_map/ppermute | solution.py:33
  436.8 1.9 collective-permute-start.6
  438.7 3.6 collective-permute-start.4
  444.4 1.9 copy.37
  447.5 3.2 collective-permute-done.4
  450.7 8.8 %collective-permute-done.5 = f32[1,128,768]{2,1,0:T(8,128)} collective-permute-done((f32[1,128,768]{2,1,0:T(8,128)}, f32[1,128,768]{2,1,0:T(8,128)}, u32[]{:S(2)}, u32[]{:S(2)}) %collective-permute-start.5) | collective-permute-done | bytes 393248 | tf_op jit(solution)/shard_map/ppermute | solution.py:33
  459.5 2.0 fusion.29
  (122 shorter events, 67.7 us)
Async XLA Ops:
  7.2 84.1 %copy-start = (bf16[768,768]{1,0:T(8,128)(2,1)S(1)}, bf16[768,768]{1,0:T(8,128)(2,1)}, u32[]{:S(2)}) copy-start(bf16[768,768]{1,0:T(8,128)(2,1)} %param.27) | copy-start | bytes 3538948
  7.9 34.2 %copy-start.13 = (s32[3]{0:T(128)S(1)}, s32[3]{0:T(128)}, u32[]{:S(2)}) copy-start(s32[3]{0:T(128)} %constant.110.clone.1) | copy-start | bytes 40
  7.9 34.2 %copy-start.16 = (s32[12]{0:T(128)S(1)}, s32[12]{0:T(128)}, u32[]{:S(2)}) copy-start(s32[12]{0:T(128)} %param.21) | copy-start | bytes 148
  7.9 34.2 %copy-start.17 = (s32[12]{0:T(128)S(1)}, s32[12]{0:T(128)}, u32[]{:S(2)}) copy-start(s32[12]{0:T(128)} %param.22) | copy-start | bytes 148
  8.9 6.6 %collective-permute-start = (bf16[1,1,1,128,768]{4,3,2,1,0:T(8,128)(2,1)S(1)}, bf16[1,1,1,128,768]{4,3,2,1,0:T(8,128)(2,1)S(1)}, u32[]{:S(2)}, u32[]{:S(2)}) collective-permute-start(bf16[1,1,1,128,768]{4,3,2,1,0:T(8,128)(2,1)S(1)} %dynamic-slice_bitcast_fusion), channel_id=1, source_target_pairs={{0,32},{32,64},{64,96},{96,128},{128,160},{160,192},{192,224},{224... | collective-permute-start | bytes 589832 | tf_op jit(solution)/shard_map/ppermute | solution.py:24
  13.0 11.5 %collective-permute-start.1 = (bf16[1,1,1,128,768]{4,3,2,1,0:T(8,128)(2,1)S(1)}, bf16[1,1,1,128,768]{4,3,2,1,0:T(8,128)(2,1)S(1)}, u32[]{:S(2)}, u32[]{:S(2)}) collective-permute-start(bf16[1,1,1,128,768]{4,3,2,1,0:T(8,128)(2,1)S(1)} %dynamic-slice_bitcast_fusion), channel_id=1, source_target_pairs={{32,0},{64,32},{96,64},{128,96},{160,128},{192,160},{224,192},{256... | collective-permute-start | bytes 589832 | tf_op jit(solution)/shard_map/ppermute | solution.py:25
  24.6 12.1 %collective-permute-start.2 = (bf16[3,1,1,128,768]{4,3,2,1,0:T(8,128)(2,1)S(1)}, bf16[3,1,1,128,768]{4,3,2,1,0:T(8,128)(2,1)S(1)}, u32[]{:S(2)}, u32[]{:S(2)}) collective-permute-start(bf16[3,1,1,128,768]{4,3,2,1,0:T(8,128)(2,1)S(1)} %pad_maximum_fusion), channel_id=1, source_target_pairs={{0,1},{1,2},{2,3},{3,4},{4,5},{5,6},{6,7},{7,8},{8,9},{9,10},{10,1... | collective-permute-start | bytes 1769480 | tf_op jit(solution)/shard_map/ppermute | solution.py:24
  30.9 11.2 %collective-permute-start.3 = (bf16[3,1,1,128,768]{4,3,2,1,0:T(8,128)(2,1)S(1)}, bf16[3,1,1,128,768]{4,3,2,1,0:T(8,128)(2,1)S(1)}, u32[]{:S(2)}, u32[]{:S(2)}) collective-permute-start(bf16[3,1,1,128,768]{4,3,2,1,0:T(8,128)(2,1)S(1)} %pad_maximum_fusion), channel_id=1, source_target_pairs={{1,0},{2,1},{3,2},{4,3},{5,4},{6,5},{7,6},{8,7},{9,8},{10,9},{11,1... | collective-permute-start | bytes 1769480 | tf_op jit(solution)/shard_map/ppermute | solution.py:25
  42.2 49.1 %copy-start.12 = (bf16[256,768]{1,0:T(8,128)(2,1)S(1)}, bf16[256,768]{1,0:T(8,128)(2,1)}, u32[]{:S(2)}) copy-start(bf16[256,768]{1,0:T(8,128)(2,1)} %param.20) | copy-start | bytes 1179652
  92.7 65.8 %copy-start.11 = (bf16[256,768]{1,0:T(8,128)(2,1)}, bf16[256,768]{1,0:T(8,128)(2,1)S(1)}, u32[]{:S(2)}) copy-start(bf16[256,768]{1,0:T(8,128)(2,1)S(1)} %get-tuple-element.171) | copy-start | bytes 1179652
  92.7 64.4 %copy-start.9 = (bf16[256,768]{1,0:T(8,128)(2,1)S(1)}, bf16[256,768]{1,0:T(8,128)(2,1)}, u32[]{:S(2)}) copy-start(bf16[256,768]{1,0:T(8,128)(2,1)} %param.29) | copy-start | bytes 1179652
  92.7 65.3 %copy-start.4 = (bf16[768,768]{1,0:T(8,128)(2,1)S(1)}, bf16[768,768]{1,0:T(8,128)(2,1)}, u32[]{:S(2)}) copy-start(bf16[768,768]{1,0:T(8,128)(2,1)} %param.28) | copy-start | bytes 3538948
  93.9 84.4 %all-to-all-start = ((bf16[32,16,768]{2,1,0:T(8,128)(2,1)}), bf16[32,16,768]{2,1,0:T(8,128)(2,1)}, u32[]{:S(2)}, u32[]{:S(2)}) async-start(bf16[32,16,768]{2,1,0:T(8,128)(2,1)} %stack.2), calls=%async_computation | async-start | bytes 1572864 | tf_op jit(solution)/shard_map/all_to_all | solution.py:78
  157.0 171.8 %reduce-scatter.2.cloned.1.call-start = ((), (), s32[]{:S(2)}) async-start(), calls=%async_computation.2 | async-start | bytes 1622016 | tf_op jit(solution)/shard_map/reduce_scatter | solution.py:102
  189.1 3.3 copy-start.2
  189.1 3.3 copy-start.6
  189.1 5.2 %copy-start.3 = (f32[12,256,512]{2,1,0:T(8,128)S(1)}, f32[12,256,512]{2,1,0:T(8,128)}, u32[]{:S(2)}) copy-start(f32[12,256,512]{2,1,0:T(8,128)} %get-tuple-element.174) | copy-start | bytes 18874372
  199.9 3.1 copy-start.5
  199.9 3.1 copy-start.10
  329.9 2.8 copy-start.7
  382.1 65.4 %collective-permute-start.7 = (f32[1,128,768]{2,1,0:T(8,128)}, f32[1,128,768]{2,1,0:T(8,128)}, u32[]{:S(2)}, u32[]{:S(2)}) collective-permute-start(f32[1,128,768]{2,1,0:T(8,128)} %get-tuple-element.166), channel_id=1, source_target_pairs={{1,0},{2,1},{3,2},{4,3},{5,4},{6,5},{7,6},{8,7},{9,8},{10,9},{11,1... | collective-permute-start | bytes 1179656 | tf_op jit(solution)/shard_map/ppermute | solution.py:33
  436.8 10.7 %collective-permute-start.6 = (f32[1,128,768]{2,1,0:T(8,128)}, f32[1,128,768]{2,1,0:T(8,128)}, u32[]{:S(2)}, u32[]{:S(2)}) collective-permute-start(f32[1,128,768]{2,1,0:T(8,128)} %get-tuple-element.167), channel_id=1, source_target_pairs={{0,1},{1,2},{2,3},{3,4},{4,5},{5,6},{6,7},{7,8},{8,9},{9,10},{10,1... | collective-permute-start | bytes 1179656 | tf_op jit(solution)/shard_map/ppermute | solution.py:33
  438.7 12.0 %collective-permute-start.4 = (f32[1,128,768]{2,1,0:T(8,128)}, f32[1,128,768]{2,1,0:T(8,128)}, u32[]{:S(2)}, u32[]{:S(2)}) collective-permute-start(f32[1,128,768]{2,1,0:T(8,128)} %get-tuple-element.168), channel_id=1, source_target_pairs={{0,32},{32,64},{64,96},{96,128},{128,160},{160,192},{192,224},{224... | collective-permute-start | bytes 1179656 | tf_op jit(solution)/shard_map/ppermute | solution.py:33
  442.4 17.1 %collective-permute-start.5 = (f32[1,128,768]{2,1,0:T(8,128)}, f32[1,128,768]{2,1,0:T(8,128)}, u32[]{:S(2)}, u32[]{:S(2)}) collective-permute-start(f32[1,128,768]{2,1,0:T(8,128)} %get-tuple-element.165), channel_id=1, source_target_pairs={{32,0},{64,32},{96,64},{128,96},{160,128},{192,160},{224,192},{256... | collective-permute-start | bytes 1179656 | tf_op jit(solution)/shard_map/ppermute | solution.py:33
  (5 other events, 6.1 us)
Sparse Core Ops, SparseCore 0:
  200.0 128.7 reduce-scatter.1
